TPU v7x, 32 devices: a whole 2x2x4 slice. The times are simulated.
32 devices in a mesh: outer: 8 (over z, x), inner: 4 (over y, core).
Axes of the slice: x: 2, y: 2, z: 4, core: 2. Of those that a mesh axis runs over, the one named last changes fastest.
Arguments:
- resid: bfloat16 [4096, 2048], P(('outer', 'inner')), may hold values from -40 to 40
- queries: bfloat16 [4096, 256], P(('outer', 'inner')), may hold values from -80 to 80
- keyvals: bfloat16 [4096, 256], P(('outer', 'inner')), may hold values from -10 to 10
- piece_order: int32 [8], replicated, may hold values from 0 to 7, each once
- out_proj: bfloat16 [256, 2048], replicated, may hold values from -0.75 to 0.75
- mlp_gain: float32 [2048], replicated, may hold values from 0.25 to 1.75
- w_gate: bfloat16 [2048, 7168], P('inner', 'outer'), may hold values from -0.125 to 0.125
- w_up: bfloat16 [2048, 7168], P('inner', 'outer'), may hold values from -0.125 to 0.125
- w_down: bfloat16 [7168, 2048], P('outer', 'inner'), may hold values from -0.0625 to 0.0625
Outputs:
- layer_out: bfloat16 [4096, 2048], P(('outer', 'inner'))
Inputs may be any that keep to these rules, and one draw needn't show every extreme that they name: `piece_order`: each of the 8 piece numbers appears once.
All inputs are finite; a program needn't handle non-finite values.
Results may differ from a plain program's by a relative error of at most 0.014.
Values may be sent and summed in bfloat16 or wider, within the bound.
A program may use at most 64 MiB of HBM per device.

v0:
```python
import jax
import jax.numpy as jnp
from jax import lax
from jax.sharding import PartitionSpec as P

HD = 128
QHEADS = 2


def passed_along(block, axis, distance):
    devices = range(lax.axis_size(axis))
    route = [(i - distance, i) for i in devices if i - distance in devices]
    return lax.ppermute(block, axis, route)


def attend(state_now, kv_part, visible, query_rows):
    running_max, running_sum, weighted = state_now
    key_rows = kv_part[:, :HD]
    value_rows = kv_part[:, HD:]
    scores = jnp.einsum(
        "rd,kd->rk", query_rows, key_rows, preferred_element_type=jnp.float32
    ) * HD ** (-0.5)
    scores = jnp.where(visible, scores, -1e30)
    new_max = jnp.maximum(running_max, jnp.max(scores, axis=1))
    weights = jnp.where(visible, jnp.exp(scores - new_max[:, None]), 0.0)
    factor = jnp.exp(running_max - new_max)
    running_sum = running_sum * factor + jnp.sum(weights, axis=1)
    weighted = weighted * factor[:, None] + jnp.dot(
        weights.astype(jnp.bfloat16), value_rows, preferred_element_type=jnp.float32
    )
    return (new_max, running_sum, weighted)


def per_device(resid, queries, keyvals, piece_order, out_proj, mlp_gain, w_gate, w_up, w_down):
    row_count = resid.shape[0]
    half_rows = row_count // 2
    gate_cols, up_cols, down_rows = (
        lax.all_gather(w_gate, "inner", axis=0, tiled=True),
        lax.all_gather(w_up, "inner", axis=0, tiled=True),
        lax.all_gather(w_down, "inner", axis=1, tiled=True),
    )
    block_pos = (
        piece_order[:, None] * half_rows + jnp.arange(half_rows, dtype=jnp.int32)[None, :]
    ).reshape(-1)
    query_pos = lax.dynamic_slice_in_dim(block_pos, lax.axis_index("inner") * row_count, row_count)
    row_pos = (query_pos[:, None] + jnp.zeros((1, QHEADS), jnp.int32)).reshape(-1)
    has_before = lax.axis_index("outer") > 0
    query_rows = queries.reshape(row_count * QHEADS, HD)
    before_kv = passed_along(keyvals, "outer", 1)
    total_rows = row_count * QHEADS
    start_state = (
        jnp.full((total_rows,), -1e30, jnp.float32),
        jnp.zeros((total_rows,), jnp.float32),
        jnp.zeros((total_rows, HD), jnp.float32),
    )
    state_now = start_state
    own_part = lax.all_gather(keyvals, "inner", axis=0, tiled=True)
    before_part = lax.all_gather(before_kv, "inner", axis=0, tiled=True)
    key_count = own_part.shape[0]
    own_visible = block_pos[None, :] <= row_pos[:, None]
    before_visible = jnp.broadcast_to(has_before, (row_pos.shape[0], key_count))
    state_now = attend(state_now, own_part, own_visible, query_rows)
    state_now = attend(state_now, before_part, before_visible, query_rows)
    running_max, running_sum, weighted = state_now
    attended = (
        (weighted / running_sum[:, None]).reshape(row_count, QHEADS * HD).astype(jnp.bfloat16)
    )
    after_attn = (
        resid.astype(jnp.float32) + jnp.dot(attended, out_proj, preferred_element_type=jnp.float32)
    ).astype(jnp.bfloat16)
    after_wide = after_attn.astype(jnp.float32)
    normed = (
        after_wide
        * lax.rsqrt(jnp.mean(after_wide * after_wide, axis=1, keepdims=True) + 1e-05)
        * mlp_gain
    ).astype(jnp.bfloat16)
    normed_part = lax.all_gather(normed, "outer", axis=0, tiled=True)
    gate = jnp.dot(normed_part, gate_cols, preferred_element_type=jnp.float32)
    upward = jnp.dot(normed_part, up_cols, preferred_element_type=jnp.float32)
    hidden = (jax.nn.silu(gate) * upward).astype(jnp.bfloat16)
    mlp_sum = lax.psum_scatter(
        jnp.dot(hidden, down_rows, preferred_element_type=jnp.float32).astype(jnp.bfloat16),
        "outer",
        scatter_dimension=0,
        tiled=True,
    ).astype(jnp.float32)
    return (after_wide + mlp_sum).astype(jnp.bfloat16)


def solution(mesh):
    placed = (
        P(("outer", "inner"), None),
        P(("outer", "inner"), None),
        P(("outer", "inner"), None),
        P(),
        P(),
        P(),
        P("inner", "outer"),
        P("inner", "outer"),
        P("outer", "inner"),
    )
    return jax.shard_map(
        per_device,
        mesh=mesh,
        in_specs=placed,
        out_specs=P(("outer", "inner"), None),
        check_vma=False,
    )
```

profile of v0, /device:TPU:0, one launch (start us, length us, event | category | flops | bytes accessed | tf_op | source)
XLA Modules:
  0.0 295.7 jit_solution(5640980260196293325)
XLA Ops:
  6.5 0.0 copy-start
  6.5 0.0 copy-start.1
  6.5 0.0 all-gather.7.cloned.1.call-start
  6.5 0.7 all-gather.7.cloned.1.call-update
  7.3 0.0 all-gather.5.cloned.1.call-start
  7.3 4.9 %collective-permute-start = (bf16[128,256]{1,0:T(8,128)(2,1)}, bf16[128,256]{1,0:T(8,128)(2,1)S(1)}, u32[]{:S(2)}, u32[]{:S(2)}) collective-permute-start(bf16[128,256]{1,0:T(8,128)(2,1)} %param.11), channel_id=1, source_target_pairs={{0,4},{4,8},{8,12},{12,16},{16,20},{20,24},{24,28},{1,5},{5,9},{9,... | collective-permute-start | bytes 196616 | tf_op jit(solution)/shard_map/ppermute | solution.py:13
  12.2 0.7 broadcast_multiply_fusion
  12.9 0.1 iota_add_fusion
  12.9 0.1 add.75
  13.0 0.1 dynamic_slice.3
  13.1 0.1 add.77
  13.2 0.2 le.16
  13.3 0.9 reshape.65
  14.2 6.0 %all_gather.18 = bf16[512,256]{1,0:T(8,128)(2,1)S(1)} all-gather(bf16[128,256]{1,0:T(8,128)(2,1)} %param.11), channel_id=1, replica_groups=mesh['outer'=8,'inner'=4] {'inner'}, dimensions={0}, use_global_device_ids=true | all-gather | bytes 327680 | tf_op jit(solution)/shard_map/all_gather | solution.py:57
  20.2 0.3 fusion.28
  20.5 0.0 copy-start.2
  20.5 0.0 collective-permute-done
  20.5 7.7 %all_gather.19 = bf16[512,256]{1,0:T(8,128)(2,1)S(1)} all-gather(bf16[128,256]{1,0:T(8,128)(2,1)S(1)} %collective-permute-done), channel_id=1, replica_groups=mesh['outer'=8,'inner'=4] {'inner'}, dimensions={0}, use_global_device_ids=true | all-gather | bytes 327680 | tf_op jit(solution)/shard_map/all_gather | solution.py:58
  28.2 0.3 fusion.29
  28.5 0.4 fusion.7
  28.9 0.3 fusion.5
  29.2 0.3 fusion.6
  29.6 0.0 copy-done
  29.6 0.0 copy-done.1
  29.6 0.4 multiply_reduce_fusion
  30.0 0.0 copy-done.2
  30.0 1.0 multiply_convert_fusion.1
  30.9 0.0 all-gather.5.cloned.1.call-update
  31.0 0.0 all-gather.9.cloned.1.call-start
  31.0 0.7 all-gather.9.cloned.1.call-update
  31.7 0.0 all-gather.11.cloned.1.call-start
  31.8 0.5 all-gather.11.cloned.1.call-update
  32.3 0.0 reduce-scatter.2.cloned.1.call-start
  32.3 12.2 %all-gather.7.cloned.1.call-done = bf16[2048,896]{1,0:T(8,128)(2,1)} async-done(((bf16[512,896]{1,0:T(8,128)(2,1)}), bf16[2048,896]{1,0:T(8,128)(2,1)}) %all-gather.7.cloned.1.call-update) | async-done | bytes 3670032 | tf_op jit(solution)/shard_map/all_gather | solution.py:38
  44.5 74.9 %all-gather.5.cloned.1.call-done = bf16[1024,2048]{1,0:T(8,128)(2,1)} async-done(((bf16[128,2048]{1,0:T(8,128)(2,1)}), bf16[1024,2048]{1,0:T(8,128)(2,1)}) %all-gather.5.cloned.1.call-update) | async-done | bytes 4194320 | tf_op jit(solution)/shard_map/all_gather | solution.py:77
  119.5 9.6 %fusion.30 = f32[1024,896]{1,0:T(8,128)} fusion(bf16[1024,2048]{1,0:T(8,128)(2,1)} %all-gather.5.cloned.1.call-done, bf16[2048,896]{1,0:T(8,128)(2,1)} %all-gather.7.cloned.1.call-done), kind=kOutput, calls=%fused_computation.47 | convolution fusion | flops 3758096384 | bytes 11534336 | tf_op jit(solution)/shard_map/dot_general | solution.py:78
  129.1 22.0 %all-gather.9.cloned.1.call-done = bf16[2048,896]{1,0:T(8,128)(2,1)} async-done(((bf16[512,896]{1,0:T(8,128)(2,1)}), bf16[2048,896]{1,0:T(8,128)(2,1)}) %all-gather.9.cloned.1.call-update) | async-done | bytes 3670032 | tf_op jit(solution)/shard_map/all_gather | solution.py:39
  151.1 32.9 %all-gather.11.cloned.1.call-done = bf16[896,2048]{1,0:T(8,128)(2,1)} async-done(((bf16[896,512]{1,0:T(8,128)(2,1)}), bf16[896,2048]{1,0:T(8,128)(2,1)}) %all-gather.11.cloned.1.call-update) | async-done | bytes 3670032 | tf_op jit(solution)/shard_map/all_gather | solution.py:40
  184.0 14.7 %convolution_convert_fusion = bf16[1024,2048]{1,0:T(8,128)(2,1)} fusion(bf16[896,2048]{1,0:T(8,128)(2,1)} %all-gather.11.cloned.1.call-done, f32[1024,896]{1,0:T(8,128)} %fusion.30, bf16[1024,2048]{1,0:T(8,128)(2,1)} %all-gather.5.cloned.1.call-done, bf16[2048,896]{1,0:T(8,128)(2,1)} %all-gather.9.cloned.1.call-done), kind=kOutput, calls=%fused_computation | convolution fusion | flops 7523794944 | bytes 19398656 | tf_op jit(solution)/shard_map/dot_general | solution.py:82
  198.8 0.0 reduce-scatter.2.cloned.1.call-update
  198.8 88.5 %reduce-scatter.2.cloned.1.call-done = bf16[128,2048]{1,0:T(8,128)(2,1)} async-done(((bf16[1024,2048]{1,0:T(8,128)(2,1)}), bf16[128,2048]{1,0:T(8,128)(2,1)}) %reduce-scatter.2.cloned.1.call-update) | async-done | bytes 524304 | tf_op jit(solution)/shard_map/reduce_scatter | solution.py:81
  287.3 1.9 add_convert_fusion
  (4 shorter events, 0.1 us)
Async XLA Ops:
  6.5 23.0 %copy-start = (bf16[256,2048]{1,0:T(8,128)(2,1)S(1)}, bf16[256,2048]{1,0:T(8,128)(2,1)}, u32[]{:S(2)}) copy-start(bf16[256,2048]{1,0:T(8,128)(2,1)} %param.13) | copy-start | bytes 3145732
  6.5 23.0 %copy-start.1 = (bf16[128,2048]{1,0:T(8,128)(2,1)S(1)}, bf16[128,2048]{1,0:T(8,128)(2,1)}, u32[]{:S(2)}) copy-start(bf16[128,2048]{1,0:T(8,128)(2,1)} %param.9) | copy-start | bytes 1572868
  6.5 38.0 %all-gather.7.cloned.1.call-start = ((), (), s32[]{:S(2)}) async-start(), calls=%async_computation.2 | async-start | bytes 4587520 | tf_op jit(solution)/shard_map/all_gather | solution.py:38
  7.3 112.2 %all-gather.5.cloned.1.call-start = ((), (), s32[]{:S(2)}) async-start(), calls=%async_computation.1 | async-start | bytes 4718592 | tf_op jit(solution)/shard_map/all_gather | solution.py:77
  7.3 13.2 %collective-permute-start = (bf16[128,256]{1,0:T(8,128)(2,1)}, bf16[128,256]{1,0:T(8,128)(2,1)S(1)}, u32[]{:S(2)}, u32[]{:S(2)}) collective-permute-start(bf16[128,256]{1,0:T(8,128)(2,1)} %param.11), channel_id=1, source_target_pairs={{0,4},{4,8},{8,12},{12,16},{16,20},{20,24},{24,28},{1,5},{5,9},{9,... | collective-permute-start | bytes 196616 | tf_op jit(solution)/shard_map/ppermute | solution.py:13
  20.5 9.5 %copy-start.2 = (f32[2048]{0:T(1024)S(1)}, f32[2048]{0:T(1024)}, u32[]{:S(2)}) copy-start(f32[2048]{0:T(1024)} %param.14) | copy-start | bytes 24580
  31.0 120.1 %all-gather.9.cloned.1.call-start = ((), (), s32[]{:S(2)}) async-start(), calls=%async_computation.3 | async-start | bytes 4587520 | tf_op jit(solution)/shard_map/all_gather | solution.py:39
  31.7 152.3 %all-gather.11.cloned.1.call-start = ((), (), s32[]{:S(2)}) async-start(), calls=%async_computation.4 | async-start | bytes 4587520 | tf_op jit(solution)/shard_map/all_gather | solution.py:40
  32.3 255.0 %reduce-scatter.2.cloned.1.call-start = ((), (), s32[]{:S(2)}) async-start(), calls=%async_computation.5 | async-start | bytes 4718592 | tf_op jit(solution)/shard_map/reduce_scatter | solution.py:81
Sparse Core Ops, SparseCore 0:
  8.9 35.6 all-gather.6
  46.7 72.7 all-gather.4
  121.1 30.0 all-gather.8
  152.5 31.4 all-gather.10
  198.9 88.3 reduce-scatter.1
where the time goes:
time: 296 us
  waiting for transfers between devices  232 us (78%)
  matrix products  26 us (9%)
  blocking collectives  13.7 us (5%)
  between operations  13.2 us (4%)
  starting transfers between devices  5.03 us (2%)
  other arithmetic  4.03 us (1%)
    reduce_scatter x1, waiting for transfers between devices, per_device(): lax.psum_scatter(jnp.dot(hidden, down_rows, preferred_element_type=jnp.fl...  88.5 us
    all_gather x1, waiting for transfers between devices, per_device(): normed_part = lax.all_gather(normed, 'outer', axis=0, tiled=True)  74.9 us
    all_gather x1, waiting for transfers between devices, per_device(): lax.all_gather(w_down, 'inner', axis=1, tiled=True)  32.9 us
    all_gather x1, waiting for transfers between devices, per_device(): lax.all_gather(w_up, 'inner', axis=0, tiled=True)  22 us
    dot_general x1, matrix products, per_device(): jnp.dot(hidden, down_rows, preferred_element_type=jnp.float32)  14.7 us
    all_gather x1, waiting for transfers between devices, per_device(): lax.all_gather(w_gate, 'inner', axis=0, tiled=True)  12.2 us
    dot_general x1, matrix products, per_device(): gate = jnp.dot(normed_part, gate_cols, preferred_element_type=jnp.float32)  9.63 us
    all_gather x1, blocking collectives, per_device(): before_part = lax.all_gather(before_kv, 'inner', axis=0, tiled=True)  7.72 us
  transfers between devices with their start and end apart: 6, of which 5 were waited for; matrix products, arithmetic and copies ran while one was open for 5% of the time, Pallas kernels for 0%

commit v1 on v0

--- a/solution.py
+++ b/solution.py
@@ -5,6 +5,17 @@
 
 HD = 128
 QHEADS = 2
+
+
+def pass_along(block, mesh_axis, dim):
+    count = lax.axis_size(mesh_axis)
+    route = [(i, (i + 1) % count) for i in range(count)]
+    shards = [block]
+    for far in range(1, count):
+        shards = [lax.ppermute(shards[0], mesh_axis, route), *shards]
+    full = jnp.concatenate(shards, axis=dim)
+    offset = (lax.axis_index(mesh_axis) + 1) * shards[-1].shape[dim]
+    return jnp.roll(full, offset, axis=dim)
 
 
 def passed_along(block, axis, distance):
@@ -74,7 +85,7 @@
         * lax.rsqrt(jnp.mean(after_wide * after_wide, axis=1, keepdims=True) + 1e-05)
         * mlp_gain
     ).astype(jnp.bfloat16)
-    normed_part = lax.all_gather(normed, "outer", axis=0, tiled=True)
+    normed_part = pass_along(normed, "outer", 0)
     gate = jnp.dot(normed_part, gate_cols, preferred_element_type=jnp.float32)
     upward = jnp.dot(normed_part, up_cols, preferred_element_type=jnp.float32)
     hidden = (jax.nn.silu(gate) * upward).astype(jnp.bfloat16)

time: 296 us -> 275 us (0.929)
  waiting for transfers between devices: 232 us -> 186 us
  local copies, waits for them, and re-layouts: 1.29 us -> 22.9 us
    ppermute x0 -> x7, waiting for transfers between devices: none -> 99 us  [pass_along(): shards = [lax.ppermute(shards[0], mesh_axis, route), *shards]]
    all_gather x1 -> x0, waiting for transfers between devices: 74.9 us -> none  [per_device(): normed_part = lax.all_gather(normed, 'outer', axis=0, tiled=True)]
    all_gather x1, waiting for transfers between devices: 32.9 us -> 0.01 us  [per_device(): lax.all_gather(w_down, 'inner', axis=1, tiled=True)]
    all_gather x1, waiting for transfers between devices: 22 us -> 0.01 us  [per_device(): lax.all_gather(w_up, 'inner', axis=0, tiled=True)]
    unnamed x6 -> x30, local copies, waits for them, and re-layouts: 0.01 us -> 21.6 us
    all_gather x1, waiting for transfers between devices: 12.2 us -> 0.01 us  [per_device(): lax.all_gather(w_gate, 'inner', axis=0, tiled=True)]
  transfers between devices with their start and end apart: 6 -> 12, of which waited for: 5 -> 8; matrix products, arithmetic and copies ran while one was open for 5% -> 13% of each run, Pallas kernels for 0% -> 0%
where the time goes in v1:
time: 275 us; the launch traced here: 274 us
  waiting for transfers between devices  186 us (68%)
  matrix products  27.1 us (10%)
  local copies, waits for them, and re-layouts  22.9 us (8%)
  blocking collectives  13.7 us (5%)
  between operations  13.3 us (5%)
  starting transfers between devices  6.64 us (2%)
  other arithmetic  5.2 us (2%)
    ppermute x7, waiting for transfers between devices, pass_along(): shards = [lax.ppermute(shards[0], mesh_axis, route), *shards]  99 us
    reduce_scatter x1, waiting for transfers between devices, per_device(): lax.psum_scatter(jnp.dot(hidden, down_rows, preferred_element_type=jnp.fl...  85.8 us
    unnamed x30, local copies, waits for them, and re-layouts  21.6 us
    dot_general x1, matrix products, per_device(): jnp.dot(hidden, down_rows, preferred_element_type=jnp.float32)  14.8 us
    dot_general x1, matrix products, per_device(): upward = jnp.dot(normed_part, up_cols, preferred_element_type=jnp.float32)  9.66 us
    all_gather x1, blocking collectives, per_device(): before_part = lax.all_gather(before_kv, 'inner', axis=0, tiled=True)  7.71 us
    all_gather x1, blocking collectives, per_device(): own_part = lax.all_gather(keyvals, 'inner', axis=0, tiled=True)  5.99 us
  transfers between devices with their start and end apart: 12, of which 8 were waited for; matrix products, arithmetic and copies ran while one was open for 13% of the time, Pallas kernels for 0%

profile of v1, /device:TPU:0, one launch (start us, length us, event | category | flops | bytes accessed | tf_op | source)
XLA Modules:
  0.0 274.4 jit_solution(17876393473443235859)
XLA Ops:
  6.5 0.7 all-gather.6.cloned.1.call-update
  7.3 0.0 all-gather.4.cloned.1.call-start
  7.3 4.9 %collective-permute-start = (bf16[128,256]{1,0:T(8,128)(2,1)}, bf16[128,256]{1,0:T(8,128)(2,1)S(1)}, u32[]{:S(2)}, u32[]{:S(2)}) collective-permute-start(bf16[128,256]{1,0:T(8,128)(2,1)} %param.11), channel_id=1, source_target_pairs={{0,4},{4,8},{8,12},{12,16},{16,20},{20,24},{24,28},{1,5},{5,9},{9,... | collective-permute-start | bytes 196616 | tf_op jit(solution)/shard_map/ppermute | solution.py:24
  12.2 0.0 all-gather.4.cloned.1.call-update
  12.2 0.0 all-gather.8.cloned.1.call-start
  12.3 6.0 %all_gather.15 = bf16[512,256]{1,0:T(8,128)(2,1)S(1)} all-gather(bf16[128,256]{1,0:T(8,128)(2,1)} %param.11), channel_id=1, replica_groups=mesh['outer'=8,'inner'=4] {'inner'}, dimensions={0}, use_global_device_ids=true | all-gather | bytes 327680 | tf_op jit(solution)/shard_map/all_gather | solution.py:68
  18.3 0.7 broadcast_multiply_fusion
  18.9 0.1 iota_add_fusion
  19.0 0.1 add.88
  19.1 0.1 dynamic_slice.7
  19.1 0.1 add.90
  19.2 0.1 le.16
  19.4 0.9 reshape.65
  20.2 0.3 fusion.40
  20.6 0.0 collective-permute-done
  20.6 7.7 %all_gather.16 = bf16[512,256]{1,0:T(8,128)(2,1)S(1)} all-gather(bf16[128,256]{1,0:T(8,128)(2,1)S(1)} %collective-permute-done), channel_id=1, replica_groups=mesh['outer'=8,'inner'=4] {'inner'}, dimensions={0}, use_global_device_ids=true | all-gather | bytes 327680 | tf_op jit(solution)/shard_map/all_gather | solution.py:69
  28.3 0.3 fusion.41
  28.6 0.4 fusion.16
  29.0 0.3 fusion.10
  29.3 0.3 fusion.11
  29.6 0.0 copy-done
  29.6 1.4 multiply_reduce_fusion
  31.1 0.2 multiply_convert_fusion.2
  31.2 1.6 collective-permute-start.1
  32.9 15.3 %collective-permute-done.1 = bf16[128,2048]{1,0:T(8,128)(2,1)S(1)} collective-permute-done((bf16[128,2048]{1,0:T(8,128)(2,1)S(1)}, bf16[128,2048]{1,0:T(8,128)(2,1)S(1)}, u32[]{:S(2)}, u32[]{:S(2)}) %collective-permute-start.1) | collective-permute-done | bytes 524320 | tf_op jit(solution)/shard_map/ppermute | solution.py:15
  48.2 0.0 collective-permute-start.2
  48.2 16.0 %collective-permute-done.2 = bf16[128,2048]{1,0:T(8,128)(2,1)S(1)} collective-permute-done((bf16[128,2048]{1,0:T(8,128)(2,1)S(1)}, bf16[128,2048]{1,0:T(8,128)(2,1)S(1)}, u32[]{:S(2)}, u32[]{:S(2)}) %collective-permute-start.2) | collective-permute-done | bytes 524320 | tf_op jit(solution)/shard_map/ppermute | solution.py:15
  64.2 0.0 collective-permute-start.3
  64.2 15.2 %collective-permute-done.3 = bf16[128,2048]{1,0:T(8,128)(2,1)S(1)} collective-permute-done((bf16[128,2048]{1,0:T(8,128)(2,1)S(1)}, bf16[128,2048]{1,0:T(8,128)(2,1)S(1)}, u32[]{:S(2)}, u32[]{:S(2)}) %collective-permute-start.3) | collective-permute-done | bytes 524320 | tf_op jit(solution)/shard_map/ppermute | solution.py:15
  79.3 0.8 copy-done.1
  80.1 0.0 collective-permute-start.4
  80.1 14.3 %collective-permute-done.4 = bf16[128,2048]{1,0:T(8,128)(2,1)S(1)} collective-permute-done((bf16[128,2048]{1,0:T(8,128)(2,1)S(1)}, bf16[128,2048]{1,0:T(8,128)(2,1)S(1)}, u32[]{:S(2)}, u32[]{:S(2)}) %collective-permute-start.4) | collective-permute-done | bytes 524320 | tf_op jit(solution)/shard_map/ppermute | solution.py:15
  94.5 0.8 copy-done.3
  95.2 0.0 collective-permute-start.5
  95.3 13.4 %collective-permute-done.5 = bf16[128,2048]{1,0:T(8,128)(2,1)S(1)} collective-permute-done((bf16[128,2048]{1,0:T(8,128)(2,1)S(1)}, bf16[128,2048]{1,0:T(8,128)(2,1)S(1)}, u32[]{:S(2)}, u32[]{:S(2)}) %collective-permute-start.5) | collective-permute-done | bytes 524320 | tf_op jit(solution)/shard_map/ppermute | solution.py:15
  108.7 0.8 copy-done.5
  109.5 0.0 collective-permute-start.6
  109.5 12.7 %collective-permute-done.6 = bf16[128,2048]{1,0:T(8,128)(2,1)} collective-permute-done((bf16[128,2048]{1,0:T(8,128)(2,1)S(1)}, bf16[128,2048]{1,0:T(8,128)(2,1)}, u32[]{:S(2)}, u32[]{:S(2)}) %collective-permute-start.6) | collective-permute-done | bytes 524320 | tf_op jit(solution)/shard_map/ppermute | solution.py:15
  122.2 0.0 collective-permute-start.7
  122.2 0.0 all-gather.8.cloned.1.call-update
  122.2 0.0 reduce-scatter.2.cloned.1.call-start
  122.3 0.0 copy-start.6
  122.3 12.1 %collective-permute-done.7 = bf16[128,2048]{1,0:T(8,128)(2,1)} collective-permute-done((bf16[128,2048]{1,0:T(8,128)(2,1)}, bf16[128,2048]{1,0:T(8,128)(2,1)}, u32[]{:S(2)}, u32[]{:S(2)}) %collective-permute-start.7) | collective-permute-done | bytes 524320 | tf_op jit(solution)/shard_map/ppermute | solution.py:15
  134.4 1.9 constant_dynamic-update-slice_fusion.15
  136.3 1.9 constant_dynamic-update-slice_fusion.14
  138.2 1.9 constant_dynamic-update-slice_fusion.13
  140.1 1.9 constant_dynamic-update-slice_fusion.12
  142.0 1.9 constant_dynamic-update-slice_fusion.11
  143.9 0.8 constant_dynamic-update-slice_fusion.10
  144.7 0.8 constant_dynamic-update-slice_fusion.9
  145.6 1.0 constant_dynamic-update-slice_fusion.8
  146.5 1.9 constant_dynamic-update-slice_fusion.7
  148.4 1.9 constant_dynamic-update-slice_fusion.6
  150.3 0.9 constant_dynamic-update-slice_fusion.5
  151.2 0.9 constant_dynamic-update-slice_fusion.4
  152.1 0.9 constant_dynamic-update-slice_fusion.3
  152.9 0.8 constant_dynamic-update-slice_fusion.2
  153.7 0.8 constant_dynamic-update-slice_fusion.1
  154.6 1.0 constant_dynamic-update-slice_fusion
  155.6 9.7 %fusion = f32[1024,896]{1,0:T(8,128)} fusion(bf16[2048,896]{1,0:T(8,128)(2,1)} %all-gather.6.cloned.1.call-done, bf16[2048,2048]{1,0:T(8,128)(2,1)} %constant_dynamic-update-slice_fusion, s32[]{:T(128)S(6)} %select_n.35), kind=kOutput, calls=%fused_computation.1 | convolution fusion | flops 3758096384 | bytes 11534340 | tf_op jit(solution)/shard_map/dot_general | solution.py:90
  165.3 14.8 %convolution_convert_fusion = bf16[1024,2048]{1,0:T(8,128)(2,1)} fusion(bf16[896,2048]{1,0:T(8,128)(2,1)} %all-gather.8.cloned.1.call-done, f32[1024,896]{1,0:T(8,128)} %fusion, bf16[2048,896]{1,0:T(8,128)(2,1)} %all-gather.4.cloned.1.call-done, bf16[2048,2048]{1,0:T(8,128)(2,1)} %constant_dynamic-update-slice_fusion, s32[]{:T(128)S(6)} %select_n.35), kind=kOutput, calls=%fused_computation | convolution fusion | flops 7523794944 | bytes 19398660 | tf_op jit(solution)/shard_map/dot_general | solution.py:93
  180.1 0.0 reduce-scatter.2.cloned.1.call-update
  180.1 85.8 %reduce-scatter.2.cloned.1.call-done = bf16[128,2048]{1,0:T(8,128)(2,1)} async-done(((bf16[1024,2048]{1,0:T(8,128)(2,1)}), bf16[128,2048]{1,0:T(8,128)(2,1)}) %reduce-scatter.2.cloned.1.call-update) | async-done | bytes 524304 | tf_op jit(solution)/shard_map/reduce_scatter | solution.py:92
  266.0 1.9 add_convert_fusion
  (19 shorter events, 0.1 us)
Async XLA Ops:
  6.5 23.1 %copy-start = (bf16[256,2048]{1,0:T(8,128)(2,1)S(1)}, bf16[256,2048]{1,0:T(8,128)(2,1)}, u32[]{:S(2)}) copy-start(bf16[256,2048]{1,0:T(8,128)(2,1)} %param.13) | copy-start | bytes 3145732
  6.5 24.5 %copy-start.7 = (f32[2048]{0:T(1024)S(1)}, f32[2048]{0:T(1024)}, u32[]{:S(2)}) copy-start(f32[2048]{0:T(1024)} %param.14) | copy-start | bytes 24580
  6.5 149.0 %all-gather.6.cloned.1.call-start = ((), (), s32[]{:S(2)}) async-start(), calls=%async_computation.2 | async-start | bytes 4587520 | tf_op jit(solution)/shard_map/all_gather | solution.py:50
  7.3 158.0 %all-gather.4.cloned.1.call-start = ((), (), s32[]{:S(2)}) async-start(), calls=%async_computation.1 | async-start | bytes 4587520 | tf_op jit(solution)/shard_map/all_gather | solution.py:49
  7.3 13.3 %collective-permute-start = (bf16[128,256]{1,0:T(8,128)(2,1)}, bf16[128,256]{1,0:T(8,128)(2,1)S(1)}, u32[]{:S(2)}, u32[]{:S(2)}) collective-permute-start(bf16[128,256]{1,0:T(8,128)(2,1)} %param.11), channel_id=1, source_target_pairs={{0,4},{4,8},{8,12},{12,16},{16,20},{20,24},{24,28},{1,5},{5,9},{9,... | collective-permute-start | bytes 196616 | tf_op jit(solution)/shard_map/ppermute | solution.py:24
  12.2 153.0 %all-gather.8.cloned.1.call-start = ((), (), s32[]{:S(2)}) async-start(), calls=%async_computation.3 | async-start | bytes 4587520 | tf_op jit(solution)/shard_map/all_gather | solution.py:51
  31.2 16.9 %collective-permute-start.1 = (bf16[128,2048]{1,0:T(8,128)(2,1)S(1)}, bf16[128,2048]{1,0:T(8,128)(2,1)S(1)}, u32[]{:S(2)}, u32[]{:S(2)}) collective-permute-start(bf16[128,2048]{1,0:T(8,128)(2,1)S(1)} %multiply_convert_fusion.2), channel_id=1, source_target_pairs={{0,4},{4,8},{8,12},{12,16},{16,20},{20,24},{24,28},{28,0},{1,5},{5... | collective-permute-start | bytes 1572872 | tf_op jit(solution)/shard_map/ppermute | solution.py:15
  48.2 16.0 %collective-permute-start.2 = (bf16[128,2048]{1,0:T(8,128)(2,1)S(1)}, bf16[128,2048]{1,0:T(8,128)(2,1)S(1)}, u32[]{:S(2)}, u32[]{:S(2)}) collective-permute-start(bf16[128,2048]{1,0:T(8,128)(2,1)S(1)} %collective-permute-done.1), channel_id=1, source_target_pairs={{0,4},{4,8},{8,12},{12,16},{16,20},{20,24},{24,28},{28,0},{1,5},{5... | collective-permute-start | bytes 1572872 | tf_op jit(solution)/shard_map/ppermute | solution.py:15
  64.2 15.2 %collective-permute-start.3 = (bf16[128,2048]{1,0:T(8,128)(2,1)S(1)}, bf16[128,2048]{1,0:T(8,128)(2,1)S(1)}, u32[]{:S(2)}, u32[]{:S(2)}) collective-permute-start(bf16[128,2048]{1,0:T(8,128)(2,1)S(1)} %collective-permute-done.2), channel_id=1, source_target_pairs={{0,4},{4,8},{8,12},{12,16},{16,20},{20,24},{24,28},{28,0},{1,5},{5... | collective-permute-start | bytes 1572872 | tf_op jit(solution)/shard_map/ppermute | solution.py:15
  79.3 0.8 copy-start.1
  80.1 14.3 %collective-permute-start.4 = (bf16[128,2048]{1,0:T(8,128)(2,1)S(1)}, bf16[128,2048]{1,0:T(8,128)(2,1)S(1)}, u32[]{:S(2)}, u32[]{:S(2)}) collective-permute-start(bf16[128,2048]{1,0:T(8,128)(2,1)S(1)} %collective-permute-done.3), channel_id=1, source_target_pairs={{0,4},{4,8},{8,12},{12,16},{16,20},{20,24},{24,28},{28,0},{1,5},{5... | collective-permute-start | bytes 1572872 | tf_op jit(solution)/shard_map/ppermute | solution.py:15
  94.5 0.8 copy-start.3
  95.2 13.4 %collective-permute-start.5 = (bf16[128,2048]{1,0:T(8,128)(2,1)S(1)}, bf16[128,2048]{1,0:T(8,128)(2,1)S(1)}, u32[]{:S(2)}, u32[]{:S(2)}) collective-permute-start(bf16[128,2048]{1,0:T(8,128)(2,1)S(1)} %collective-permute-done.4), channel_id=1, source_target_pairs={{0,4},{4,8},{8,12},{12,16},{16,20},{20,24},{24,28},{28,0},{1,5},{5... | collective-permute-start | bytes 1572872 | tf_op jit(solution)/shard_map/ppermute | solution.py:15
  108.7 0.8 copy-start.5
  109.5 12.7 %collective-permute-start.6 = (bf16[128,2048]{1,0:T(8,128)(2,1)S(1)}, bf16[128,2048]{1,0:T(8,128)(2,1)}, u32[]{:S(2)}, u32[]{:S(2)}) collective-permute-start(bf16[128,2048]{1,0:T(8,128)(2,1)S(1)} %collective-permute-done.5), channel_id=1, source_target_pairs={{0,4},{4,8},{8,12},{12,16},{16,20},{20,24},{24,28},{28,0},{1,5},{5... | collective-permute-start | bytes 1572872 | tf_op jit(solution)/shard_map/ppermute | solution.py:15
  122.2 12.2 %collective-permute-start.7 = (bf16[128,2048]{1,0:T(8,128)(2,1)}, bf16[128,2048]{1,0:T(8,128)(2,1)}, u32[]{:S(2)}, u32[]{:S(2)}) collective-permute-start(bf16[128,2048]{1,0:T(8,128)(2,1)} %collective-permute-done.6), channel_id=1, source_target_pairs={{0,4},{4,8},{8,12},{12,16},{16,20},{20,24},{24,28},{28,0},{1,5},{5... | collective-permute-start | bytes 1572872 | tf_op jit(solution)/shard_map/ppermute | solution.py:15
  122.2 143.7 %reduce-scatter.2.cloned.1.call-start = ((), (), s32[]{:S(2)}) async-start(), calls=%async_computation.4 | async-start | bytes 4718592 | tf_op jit(solution)/shard_map/reduce_scatter | solution.py:92
  122.3 28.0 %copy-start.6 = (bf16[128,2048]{1,0:T(8,128)(2,1)S(1)}, bf16[128,2048]{1,0:T(8,128)(2,1)}, u32[]{:S(2)}) copy-start(bf16[128,2048]{1,0:T(8,128)(2,1)} %copy-done.5) | copy-start | bytes 1572868
  122.3 28.9 %copy-start.4 = (bf16[128,2048]{1,0:T(8,128)(2,1)S(1)}, bf16[128,2048]{1,0:T(8,128)(2,1)}, u32[]{:S(2)}) copy-start(bf16[128,2048]{1,0:T(8,128)(2,1)} %copy-done.3) | copy-start | bytes 1572868
  122.3 29.8 %copy-start.2 = (bf16[128,2048]{1,0:T(8,128)(2,1)S(1)}, bf16[128,2048]{1,0:T(8,128)(2,1)}, u32[]{:S(2)}) copy-start(bf16[128,2048]{1,0:T(8,128)(2,1)} %copy-done.1) | copy-start | bytes 1572868
Sparse Core Ops, SparseCore 0:
  8.9 35.6 all-gather.5
  46.1 31.4 all-gather.3
  122.3 32.9 all-gather.7
  180.2 85.6 reduce-scatter.1
